TPU v7x, 128 devices: a whole 4x4x4 slice. The times are simulated.
128 devices in a mesh: row: 8 (over z, core), col: 16 (over y, x).
Axes of the slice: x: 4, y: 4, z: 4, core: 2. Of those that a mesh axis runs over, the one named last changes fastest.
Arguments:
- right_side: float32 [8, 65536], P(None, ('row', 'col')), may hold values from -30 to 30
- u_factors: bfloat16 [128, 128, 48, 512], P(('row', 'col')), may hold values from -0.078125 to 0.078125
- v_factors: bfloat16 [128, 128, 48, 512], P('row', 'col'), may hold values from -0.25 to 0.25
- ranks: int32 [128, 128], P('row', 'col'), may hold values from 8 to 48
- far_blocks: bfloat16 [16, 512, 65536], P('row', None, 'col'), may hold values from -0.09375 to 0.09375
- block_target: int32 [16, 16], replicated, may hold values from 0 to 127, as said below
- recv_order: int32 [128], replicated, may hold values from 0 to 127, as said below
Outputs:
- densities: float32 [8, 65536], P(None, 'col')
- residual: float32 [8, 65536], P(None, ('row', 'col'))
- far_field: float32 [128, 4096], P(('row', 'col'))
Inputs may be any that keep to these rules, and one draw needn't show every extreme that they name: `recv_order`: a permutation of the receiver patches. `block_target`: block (b, c) with b % 2 == 0 lies on device g = (b // 2) * 16 + c; its receiver patch is stored in output rows owned by device (g + 128 / 2) mod 128 if g is even and by device g - 1 if g is odd; the other blocks may name any receiver patch.
All inputs are finite; a program needn't handle non-finite values.
Results may differ from a plain program's by a relative error of at most 0.008.
Values may be sent and summed in bfloat16 or wider, within the bound.
No kernel may reach another device: no remote copies, remote signals or barrier semaphores. Data moves between devices by JAX's collectives and lax.ppermute only.
A program may use at most 128 MiB of HBM per device.

v0:
```python
import jax
import jax.numpy as jnp
from jax import lax
from jax.sharding import PartitionSpec as P

ITERS = 2


def per_device(right_side, u_factors, v_factors, ranks, far_blocks, block_target, recv_order):
    dens_count = right_side.shape[0]
    own_rows = u_factors.shape[0]
    all_cols = u_factors.shape[1]
    slot_count = u_factors.shape[2]
    patch_len = u_factors.shape[3]
    group_rows = v_factors.shape[0]
    own_cols = v_factors.shape[1]
    slot_index = lax.broadcasted_iota(jnp.int32, (group_rows, own_cols, slot_count, 1), 2)
    kept = (slot_index < ranks[:, :, None, None]).astype(jnp.float32)
    kept_half = kept.astype(jnp.bfloat16)
    residual = right_side
    densities = jnp.zeros((dens_count, own_cols * patch_len), jnp.float32)
    for iteration in range(ITERS):
        res_bf = residual.astype(jnp.bfloat16).reshape(dens_count, own_rows, patch_len)
        back_coef = jnp.einsum(
            "ijsp,dip->ijsd", u_factors, res_bf, preferred_element_type=jnp.float32
        )
        back_coef = back_coef.astype(jnp.bfloat16).reshape(
            own_rows, all_cols, slot_count * dens_count
        )
        arrived = lax.all_to_all(back_coef, "col", split_axis=1, concat_axis=0, tiled=True)
        arrived = arrived.reshape(group_rows, own_cols, slot_count, dens_count) * kept_half
        partial_grad = jnp.einsum(
            "ijsp,ijsd->djp", v_factors, arrived, preferred_element_type=jnp.float32
        )
        grad = lax.psum(partial_grad.reshape(dens_count, own_cols * patch_len), "row")
        grad_local = jnp.sum(grad * grad, axis=1)
        grad_sq = lax.psum(grad_local, "col")
        grad_bf = grad.astype(jnp.bfloat16).reshape(dens_count, own_cols, patch_len)
        coefficients = (
            jnp.einsum("ijsp,djp->ijsd", v_factors, grad_bf, preferred_element_type=jnp.float32)
            * kept
        )
        coefficients = coefficients.astype(jnp.bfloat16).reshape(
            group_rows, own_cols, slot_count * dens_count
        )
        landed = lax.all_to_all(coefficients, "col", split_axis=0, concat_axis=1, tiled=True)
        landed = landed.reshape(own_rows, all_cols, slot_count, dens_count)
        image = jnp.einsum("ijsp,ijsd->dip", u_factors, landed, preferred_element_type=jnp.float32)
        image = image.reshape(dens_count, own_rows * patch_len)
        image_local = jnp.sum(image * image, axis=1)
        image_sq = lax.psum(image_local, ("row", "col"))
        step_size = grad_sq / (image_sq + 1e-06)
        densities = densities + step_size[:, None] * grad
        residual = residual - step_size[:, None] * image
    block_count = far_blocks.shape[0]
    x_half = densities.astype(jnp.bfloat16)
    block_field = jnp.einsum("bpn,dn->bdp", far_blocks, x_half, preferred_element_type=jnp.float32)
    block_field = block_field.reshape(block_count, dens_count * patch_len)
    local_target = lax.dynamic_slice(
        block_target, (lax.axis_index("row") * block_count, lax.axis_index("col")), (block_count, 1)
    ).reshape(block_count)
    onehot = (local_target[:, None] == recv_order[None, :]).astype(jnp.float32)
    far_field = lax.psum_scatter(
        jnp.dot(
            onehot.T,
            block_field,
            preferred_element_type=jnp.float32,
            precision=lax.Precision.HIGHEST,
        ),
        ("row", "col"),
        scatter_dimension=0,
        tiled=True,
    )
    return (densities, residual, far_field)


def solution(mesh):
    return jax.shard_map(
        per_device,
        mesh=mesh,
        in_specs=(
            P(None, ("row", "col")),
            P(("row", "col"), None, None, None),
            P("row", "col", None, None),
            P("row", "col"),
            P("row", None, "col"),
            P(),
            P(),
        ),
        out_specs=(P(None, "col"), P(None, ("row", "col")), P(("row", "col"), None)),
        check_vma=False,
    )
```

profile of v0, /device:TPU:1, one launch (start us, length us, event | category | flops | bytes accessed | tf_op | source)
XLA Modules:
  0.0 595.4 jit_solution(9957855549774173676)
XLA Ops:
  7.2 0.0 copy-start
  7.2 0.0 copy-start.5
  7.2 5.9 convolution_convert_fusion
  13.1 0.2 copy.50
  13.3 0.2 copy.51
  13.5 0.5 broadcast.22
  14.0 1.2 reduce.6
  15.2 0.7 reshape.129
  15.9 7.6 %all-to-all-start = ((bf16[16,2,1536]{2,1,0:T(2,128)(2,1)}), bf16[16,2,1536]{2,1,0:T(2,128)(2,1)S(1)}, u32[]{:S(2)}, u32[]{:S(2)}) async-start(bf16[16,2,1536]{2,1,0:T(2,128)(2,1)} %reshape.129), calls=%async_computation | async-start | bytes 196608 | tf_op jit(solution)/shard_map/all_to_all | solution.py:30
  23.5 0.0 all-reduce.5.cloned.1.call-start
  23.5 0.0 copy-done.5
  23.6 0.1 fusion.38
  23.7 6.6 %all-to-all-done = bf16[16,2,1536]{2,1,0:T(2,128)(2,1)S(1)} async-done(((bf16[16,2,1536]{2,1,0:T(2,128)(2,1)}), bf16[16,2,1536]{2,1,0:T(2,128)(2,1)S(1)}, u32[]{:S(2)}, u32[]{:S(2)}) %all-to-all-start) | async-done | bytes 98336 | tf_op jit(solution)/shard_map/all_to_all | solution.py:30
  30.2 0.1 reshape.130
  30.3 0.6 bitcast_reduce_fusion.1
  30.9 1.8 reshape.105
  32.6 4.8 fusion.8
  37.4 0.0 all-reduce.5.cloned.1.call-update
  37.4 58.2 %all-reduce.5.cloned.1.call-done = f32[8,4096]{1,0:T(8,128)} async-done(((f32[8,4096]{1,0:T(8,128)}), f32[8,4096]{1,0:T(8,128)}) %all-reduce.5.cloned.1.call-update) | async-done | bytes 131088 | tf_op jit(solution)/shard_map/psum | solution.py:35
  95.6 1.1 multiply_reduce_fusion.1
  96.7 5.9 fusion.22
  102.6 0.5 copy.55
  103.1 0.9 copy.56
  104.1 6.5 %all-to-all-start.1 = ((bf16[16,8,384]{2,1,0:T(8,128)(2,1)}), bf16[16,8,384]{2,1,0:T(8,128)(2,1)S(1)}, u32[]{:S(2)}, u32[]{:S(2)}) async-start(bf16[16,8,384]{2,1,0:T(8,128)(2,1)} %copy.56), calls=%async_computation.1 | async-start | bytes 196608 | tf_op jit(solution)/shard_map/all_to_all | solution.py:46
  110.6 0.0 all-reduce.7.cloned.1.call-start
  110.6 33.3 %psum.43 = f32[8]{0:T(128)S(1)} all-reduce(f32[8]{0:T(128)S(1)} %get-tuple-element.5), channel_id=1, replica_groups=mesh['row'=8,'col'=16] {'col'}, use_global_device_ids=true, to_apply=%region_2.0 | all-reduce | flops 8 | bytes 64 | tf_op jit(solution)/shard_map/psum | solution.py:37
  144.0 0.0 all-to-all-done.1
  144.0 1.8 reshape.109
  145.8 3.8 multiply_reduce_fusion.3
  149.6 72.1 %psum.44 = f32[8]{0:T(128)S(1)} all-reduce(f32[8]{0:T(128)S(1)} %get-tuple-element.9), channel_id=1, replica_groups=mesh['row'=8,'col'=16] {'row','col'}, use_global_device_ids=true, to_apply=%region_4.0 | all-reduce | flops 8 | bytes 64 | tf_op jit(solution)/shard_map/psum | solution.py:51
  221.7 0.0 copy-done.4
  221.7 9.4 %fusion.31 = bf16[1,128,384]{1,2,0:T(8,128)(2,1)S(1)} fusion(bf16[128,48,512]{2,1,0:T(8,128)(2,1)} %bitcast.81, f32[8,512]{1,0:T(8,128)S(1)} %copy-done.4, f32[8,512]{1,0:T(8,128)S(1)} %get-tuple-element.10, f32[8]{0:T(128)S(1)} %add_divide_fusion.1), kind=kOutput, calls=%fused_computation.18 | convolution fusion | flops 50393088 | bytes 6422560 | tf_op jit(solution)/shard_map/ijsp,dip->ijsd/dot_general | solution.py:24
  231.1 0.2 copy.59
  231.3 1.2 reduce.7
  232.6 10.2 %all_to_all.16 = bf16[16,2,1536]{2,1,0:T(2,128)(2,1)S(1)} all-to-all(bf16[16,2,1536]{2,1,0:T(2,128)(2,1)S(1)} %reshape.131), channel_id=1, replica_groups=mesh['row'=8,'col'=16] {'col'}, dimensions={0} | all-to-all | bytes 196608 | tf_op jit(solution)/shard_map/all_to_all | solution.py:30
  242.8 0.1 reshape.132
  242.9 0.6 bitcast_reduce_fusion
  243.5 1.8 reshape.111
  245.2 4.8 fusion.6
  250.0 0.0 all-reduce.7.cloned.1.call-update
  250.1 55.2 %all-reduce.7.cloned.1.call-done = f32[8,4096]{1,0:T(8,128)} async-done(((f32[8,4096]{1,0:T(8,128)}), f32[8,4096]{1,0:T(8,128)}) %all-reduce.7.cloned.1.call-update) | async-done | bytes 131088 | tf_op jit(solution)/shard_map/psum | solution.py:35
  305.3 1.1 fusion.51
  306.4 5.9 fusion.25
  312.3 0.5 copy.62
  312.8 0.9 copy.63
  313.7 6.5 %all-to-all-start.3 = ((bf16[16,8,384]{2,1,0:T(8,128)(2,1)}), bf16[16,8,384]{2,1,0:T(8,128)(2,1)S(1)}, u32[]{:S(2)}, u32[]{:S(2)}) async-start(bf16[16,8,384]{2,1,0:T(8,128)(2,1)} %copy.63), calls=%async_computation.3 | async-start | bytes 196608 | tf_op jit(solution)/shard_map/all_to_all | solution.py:46
  320.3 0.0 all-reduce.9.cloned.1.call-start
  320.3 0.0 copy-done
  320.3 0.2 dynamic-slice_reduce_fusion
  320.5 33.2 %psum.46 = f32[8]{0:T(128)S(1)} all-reduce(f32[8]{0:T(128)S(1)} %get-tuple-element.4), channel_id=1, replica_groups=mesh['row'=8,'col'=16] {'col'}, use_global_device_ids=true, to_apply=%region_7.0 | all-reduce | flops 8 | bytes 64 | tf_op jit(solution)/shard_map/psum | solution.py:37
  353.8 0.0 all-to-all-done.3
  353.8 1.8 reshape.115
  355.5 3.8 multiply_reduce_fusion.2
  359.4 0.0 copy-start.6
  359.4 72.0 %psum.47 = f32[8]{0:T(128)S(1)} all-reduce(f32[8]{0:T(128)S(1)} %get-tuple-element.11), channel_id=1, replica_groups=mesh['row'=8,'col'=16] {'row','col'}, use_global_device_ids=true, to_apply=%region_9.0 | all-reduce | flops 8 | bytes 64 | tf_op jit(solution)/shard_map/psum | solution.py:51
  431.4 0.0 copy-done.2
  431.4 0.1 multiply_add_fusion
  431.5 0.0 copy-start.1
  431.5 5.7 convolution_bitcast_fusion
  437.3 2.4 fusion.44
  439.7 0.0 all-reduce.9.cloned.1.call-update
  439.7 0.7 multiply_subtract_fusion
  440.4 146.9 %all-reduce.9.cloned.1.call-done = f32[128,4096]{1,0:T(8,128)} async-done(((f32[128,4096]{1,0:T(8,128)}), f32[128,4096]{1,0:T(8,128)}) %all-reduce.9.cloned.1.call-update) | async-done | bytes 2097168
  587.3 1.5 constant_dynamic-slice_fusion
  (11 shorter events, 0.1 us)
Async XLA Ops:
  7.2 313.2 %copy-start = (s32[16,16]{1,0:T(8,128)S(1)}, s32[16,16]{1,0:T(8,128)}, u32[]{:S(2)}) copy-start(s32[16,16]{1,0:T(8,128)} %param.12) | copy-start | bytes 3076
  7.2 16.4 %copy-start.5 = (s32[16,8]{0,1:T(8,128)S(1)}, s32[16,8]{0,1:T(8,128)}, u32[]{:S(2)}) copy-start(s32[16,8]{0,1:T(8,128)} %param.10) | copy-start | bytes 1540
  15.9 14.3 %all-to-all-start = ((bf16[16,2,1536]{2,1,0:T(2,128)(2,1)}), bf16[16,2,1536]{2,1,0:T(2,128)(2,1)S(1)}, u32[]{:S(2)}, u32[]{:S(2)}) async-start(bf16[16,2,1536]{2,1,0:T(2,128)(2,1)} %reshape.129), calls=%async_computation | async-start | bytes 196608 | tf_op jit(solution)/shard_map/all_to_all | solution.py:30
  23.5 72.1 %all-reduce.5.cloned.1.call-start = ((), (), s32[]{:S(2)}) async-start(), calls=%async_computation.4 | async-start | bytes 262144 | tf_op jit(solution)/shard_map/psum | solution.py:35
  102.6 119.1 %copy-start.4 = (f32[8,512]{1,0:T(8,128)S(1)}, f32[8,512]{1,0:T(8,128)}, u32[]{:S(2)}) copy-start(f32[8,512]{1,0:T(8,128)} %param.7) | copy-start | bytes 49156
  104.1 39.9 %all-to-all-start.1 = ((bf16[16,8,384]{2,1,0:T(8,128)(2,1)}), bf16[16,8,384]{2,1,0:T(8,128)(2,1)S(1)}, u32[]{:S(2)}, u32[]{:S(2)}) async-start(bf16[16,8,384]{2,1,0:T(8,128)(2,1)} %copy.56), calls=%async_computation.1 | async-start | bytes 196608 | tf_op jit(solution)/shard_map/all_to_all | solution.py:46
  110.6 194.7 %all-reduce.7.cloned.1.call-start = ((), (), s32[]{:S(2)}) async-start(), calls=%async_computation.5 | async-start | bytes 262144 | tf_op jit(solution)/shard_map/psum | solution.py:35
  312.3 119.2 %copy-start.2 = (f32[8,4096]{1,0:T(8,128)S(1)}, f32[8,4096]{1,0:T(8,128)}, u32[]{:S(2)}) copy-start(f32[8,4096]{1,0:T(8,128)} %all-reduce.5.cloned.1.call-done) | copy-start | bytes 393220
  312.3 119.2 %copy-start.3 = (f32[8,4096]{1,0:T(8,128)S(1)}, f32[8,4096]{1,0:T(8,128)}, u32[]{:S(2)}) copy-start(f32[8,4096]{1,0:T(8,128)} %all-reduce.7.cloned.1.call-done) | copy-start | bytes 393220
  313.7 40.0 %all-to-all-start.3 = ((bf16[16,8,384]{2,1,0:T(8,128)(2,1)}), bf16[16,8,384]{2,1,0:T(8,128)(2,1)S(1)}, u32[]{:S(2)}, u32[]{:S(2)}) async-start(bf16[16,8,384]{2,1,0:T(8,128)(2,1)} %copy.63), calls=%async_computation.3 | async-start | bytes 196608 | tf_op jit(solution)/shard_map/all_to_all | solution.py:46
  320.3 267.1 %all-reduce.9.cloned.1.call-start = ((), (), s32[]{:S(2)}) async-start(), calls=%async_computation.6 | async-start | bytes 4194304
  359.4 77.9 %copy-start.6 = (s32[128]{0:T(128)S(1)}, s32[128]{0:T(128)}, u32[]{:S(2)}) copy-start(s32[128]{0:T(128)} %param.13) | copy-start | bytes 1540
  431.5 8.2 %copy-start.1 = (f32[8,4096]{1,0:T(8,128)}, f32[8,4096]{1,0:T(8,128)S(1)}, u32[]{:S(2)}) copy-start(f32[8,4096]{1,0:T(8,128)S(1)} %multiply_add_fusion) | copy-start | bytes 393220
Sparse Core Ops, SparseCore 0:
  37.6 58.0 all-reduce.4
  250.2 55.0 all-reduce.6
  439.8 147.4 all-reduce.8
where the time goes:
time: 596 us; the launch traced here: 595 us
  waiting for transfers between devices  267 us (45%)
  blocking collectives  221 us (37%)
  matrix products  52.3 us (9%)
  starting transfers between devices  20.8 us (3%)
  local copies, waits for them, and re-layouts  15 us (3%)
  between operations  14 us (2%)
    unnamed x4, waiting for transfers between devices  147 us
    psum x2, blocking collectives, per_device(): image_sq = lax.psum(image_local, ('row', 'col'))  144 us
    psum x2, waiting for transfers between devices, per_device(): lax.psum(partial_grad.reshape(dens_count, own_cols * patch_len), 'row')  113 us
    psum x2, blocking collectives, per_device(): grad_sq = lax.psum(grad_local, 'col')  66.6 us
    dot_general x2, matrix products, per_device(): jnp.einsum('ijsp,dip->ijsd', u_factors, res_bf, preferred_element_type=jn...  15.3 us
    all_to_all x2, starting transfers between devices, per_device(): lax.all_to_all(coefficients, 'col', split_axis=0, concat_axis=1, tiled=True)  13.1 us
  transfers between devices with their start and end apart: 6, of which 4 were waited for; matrix products, arithmetic and copies ran while one was open for 0% of the time, Pallas kernels for 0%

commit v1 on v0

--- a/solution.py
+++ b/solution.py
@@ -48,7 +48,7 @@
         image = jnp.einsum("ijsp,ijsd->dip", u_factors, landed, preferred_element_type=jnp.float32)
         image = image.reshape(dens_count, own_rows * patch_len)
         image_local = jnp.sum(image * image, axis=1)
-        image_sq = lax.psum(image_local, ("row", "col"))
+        image_sq = lax.psum(lax.psum(image_local, "row"), "col")
         step_size = grad_sq / (image_sq + 1e-06)
         densities = densities + step_size[:, None] * grad
         residual = residual - step_size[:, None] * image

time: 596 us -> 499 us (0.84)
  blocking collectives: 221 us -> 114 us
  waiting for transfers between devices: 267 us -> 284 us
  starting transfers between devices: 20.8 us -> 14.2 us
    psum x2, blocking collectives: 144 us -> 32.2 us  [per_device(): image_sq = lax.psum(lax.psum(image_local, 'row'), 'col')]
    all_to_all x0 -> x1, blocking collectives: none -> 13 us  [per_device(): lax.all_to_all(coefficients, 'col', split_axis=0, concat_axis=1, tiled=True)]
    psum x2, blocking collectives: 66.6 us -> 59.9 us  [per_device(): grad_sq = lax.psum(grad_local, 'col')]
    all_to_all x2 -> x1, starting transfers between devices: 13.1 us -> 6.53 us  [per_device(): lax.all_to_all(coefficients, 'col', split_axis=0, concat_axis=1, tiled=True)]
    all_to_all x2 -> x1, waiting for transfers between devices: 0.01 us -> 6.41 us  [per_device(): lax.all_to_all(coefficients, 'col', split_axis=0, concat_axis=1, tiled=True)]
    psum x2, waiting for transfers between devices: 113 us -> 120 us  [per_device(): lax.psum(partial_grad.reshape(dens_count, own_cols * patch_len), 'row')]
  transfers between devices with their start and end apart: 6 -> 5, of which waited for: 4 -> 5; matrix products, arithmetic and copies ran while one was open for 0% -> 0% of each run, Pallas kernels for 0% -> 0%
where the time goes in v1:
time: 499 us
  waiting for transfers between devices  284 us (57%)
  blocking collectives  114 us (23%)
  matrix products  52.3 us (10%)
  local copies, waits for them, and re-layouts  14.3 us (3%)
  starting transfers between devices  14.2 us (3%)
  between operations  14 us (3%)
  other arithmetic  5.57 us (1%)
    unnamed x4, waiting for transfers between devices  151 us
    psum x2, waiting for transfers between devices, per_device(): lax.psum(partial_grad.reshape(dens_count, own_cols * patch_len), 'row')  120 us
    psum x2, blocking collectives, per_device(): grad_sq = lax.psum(grad_local, 'col')  59.9 us
    psum x2, blocking collectives, per_device(): image_sq = lax.psum(lax.psum(image_local, 'row'), 'col')  32.2 us
    dot_general x2, matrix products, per_device(): jnp.einsum('ijsp,dip->ijsd', u_factors, res_bf, preferred_element_type=jn...  15.3 us
    all_to_all x1, blocking collectives, per_device(): lax.all_to_all(coefficients, 'col', split_axis=0, concat_axis=1, tiled=True)  13 us
    dot_general x2, matrix products, per_device(): jnp.einsum('ijsp,djp->ijsd', v_factors, grad_bf, preferred_element_type=j...  11.7 us
  transfers between devices with their start and end apart: 5, of which 5 were waited for; matrix products, arithmetic and copies ran while one was open for 0% of the time, Pallas kernels for 0%

profile of v1, /device:TPU:1, one launch (start us, length us, event | category | flops | bytes accessed | tf_op | source)
XLA Modules:
  0.0 498.7 jit_solution(7183978598800965525)
XLA Ops:
  7.2 0.0 copy-start
  7.2 0.0 copy-start.5
  7.2 5.9 %convolution_convert_fusion = bf16[128,48,8]{1,2,0:T(8,128)(2,1)S(1)} fusion(f32[8,512]{1,0:T(8,128)} %param.7, bf16[1,128,48,512]{3,2,1,0:T(8,128)(2,1)} %param.8), kind=kOutput, calls=%fused_computation.14 | convolution fusion | flops 50384896 | bytes 6406144 | tf_op jit(solution)/shard_map/ijsp,dip->ijsd/dot_general | solution.py:24
  13.1 0.2 copy.50
  13.3 0.2 copy.51
  13.5 0.5 broadcast.22
  14.0 1.2 reduce.6
  15.2 0.7 reshape.129
  15.9 7.6 %all-to-all-start = ((bf16[16,2,1536]{2,1,0:T(2,128)(2,1)}), bf16[16,2,1536]{2,1,0:T(2,128)(2,1)S(1)}, u32[]{:S(2)}, u32[]{:S(2)}) async-start(bf16[16,2,1536]{2,1,0:T(2,128)(2,1)} %reshape.129), calls=%async_computation | async-start | bytes 196608 | tf_op jit(solution)/shard_map/all_to_all | solution.py:30
  23.5 0.0 all-reduce.7.cloned.1.call-start
  23.5 0.0 copy-done.5
  23.6 0.1 fusion.38
  23.7 6.6 %all-to-all-done = bf16[16,2,1536]{2,1,0:T(2,128)(2,1)S(1)} async-done(((bf16[16,2,1536]{2,1,0:T(2,128)(2,1)}), bf16[16,2,1536]{2,1,0:T(2,128)(2,1)S(1)}, u32[]{:S(2)}, u32[]{:S(2)}) %all-to-all-start) | async-done | bytes 98336 | tf_op jit(solution)/shard_map/all_to_all | solution.py:30
  30.2 0.1 reshape.130
  30.3 0.6 bitcast_reduce_fusion.1
  30.9 1.8 reshape.105
  32.6 4.8 fusion.8
  37.4 0.0 all-reduce.7.cloned.1.call-update
  37.4 0.0 all-reduce.9.cloned.1.call-start
  37.5 58.1 %all-reduce.7.cloned.1.call-done = f32[8,4096]{1,0:T(8,128)} async-done(((f32[8,4096]{1,0:T(8,128)}), f32[8,4096]{1,0:T(8,128)}) %all-reduce.7.cloned.1.call-update) | async-done | bytes 131088 | tf_op jit(solution)/shard_map/psum | solution.py:35
  95.6 1.1 multiply_reduce_fusion.1
  96.7 5.9 %fusion.22 = bf16[16,8,48,8]{2,3,0,1:T(8,128)(2,1)S(1)} fusion(bf16[8,8,512,1]{2,0,3,1:T(8,128)(2,1)S(1)} %bitcast.89, bf16[16,8,48,512]{3,2,1,0:T(8,128)(2,1)} %param.9, f32[16,8,48]{2,0,1:T(8,128)S(1)} %get-tuple-element.11), kind=kOutput, calls=%fused_computation.15 | convolution fusion | flops 50429952 | bytes 6479872 | tf_op jit(solution)/shard_map/ijsp,djp->ijsd/dot_general | solution.py:40
  102.6 0.5 copy.55
  103.1 0.3 copy.56
  103.4 13.0 %all_to_all.16 = bf16[16,8,384]{2,1,0:T(8,128)(2,1)S(1)} all-to-all(bf16[16,8,384]{2,1,0:T(8,128)(2,1)S(1)} %copy.56), channel_id=1, replica_groups=mesh['row'=8,'col'=16] {'col'}, dimensions={0} | all-to-all | bytes 196608 | tf_op jit(solution)/shard_map/all_to_all | solution.py:46
  116.4 1.8 reshape.109
  118.2 3.8 multiply_reduce_fusion.3
  122.1 16.1 %psum.58 = f32[8]{0:T(128)S(1)} all-reduce(f32[8]{0:T(128)S(1)} %get-tuple-element.13), channel_id=1, replica_groups=mesh['row'=8,'col'=16] {'row'}, use_global_device_ids=true, to_apply=%region_4.0 | all-reduce | flops 8 | bytes 64 | tf_op jit(solution)/shard_map/psum | solution.py:51
  138.2 30.0 %all-reduce.2 = (f32[8]{0:T(128)S(1)}, f32[8]{0:T(128)S(1)}) all-reduce(f32[8]{0:T(128)S(1)} %get-tuple-element.9, f32[8]{0:T(128)S(1)} %psum.58), channel_id=1, replica_groups=mesh['row'=8,'col'=16] {'col'}, use_global_device_ids=true, to_apply=%region_2.0 | all-reduce | flops 16 | bytes 128 | tf_op jit(solution)/shard_map/psum | solution.py:37
  168.2 0.0 copy-done.4
  168.2 9.4 %fusion.31 = bf16[1,128,384]{1,2,0:T(8,128)(2,1)S(1)} fusion(bf16[128,48,512]{2,1,0:T(8,128)(2,1)} %bitcast.81, f32[8,512]{1,0:T(8,128)S(1)} %copy-done.4, f32[8,512]{1,0:T(8,128)S(1)} %get-tuple-element.14, f32[8]{0:T(128)S(1)} %add_divide_fusion.1), kind=kOutput, calls=%fused_computation.18 | convolution fusion | flops 50393088 | bytes 6422560 | tf_op jit(solution)/shard_map/ijsp,dip->ijsd/dot_general | solution.py:24
  177.6 0.2 copy.59
  177.8 1.2 reduce.7
  179.1 9.2 %all_to_all.17 = bf16[16,2,1536]{2,1,0:T(2,128)(2,1)S(1)} all-to-all(bf16[16,2,1536]{2,1,0:T(2,128)(2,1)S(1)} %reshape.131), channel_id=1, replica_groups=mesh['row'=8,'col'=16] {'col'}, dimensions={0} | all-to-all | bytes 196608 | tf_op jit(solution)/shard_map/all_to_all | solution.py:30
  188.3 0.1 reshape.132
  188.4 0.6 bitcast_reduce_fusion
  189.0 1.8 reshape.111
  190.8 4.8 fusion.6
  195.6 0.0 all-reduce.9.cloned.1.call-update
  195.6 61.6 %all-reduce.9.cloned.1.call-done = f32[8,4096]{1,0:T(8,128)} async-done(((f32[8,4096]{1,0:T(8,128)}), f32[8,4096]{1,0:T(8,128)}) %all-reduce.9.cloned.1.call-update) | async-done | bytes 131088 | tf_op jit(solution)/shard_map/psum | solution.py:35
  257.2 1.1 fusion.51
  258.3 5.9 %fusion.25 = bf16[16,8,48,8]{2,3,0,1:T(8,128)(2,1)S(1)} fusion(bf16[8,8,512,1]{2,0,3,1:T(8,128)(2,1)S(1)} %bitcast.90, bf16[16,8,48,512]{3,2,1,0:T(8,128)(2,1)} %param.9, f32[16,8,48]{2,0,1:T(8,128)S(1)} %get-tuple-element.11), kind=kOutput, calls=%fused_computation.16 | convolution fusion | flops 50429952 | bytes 6479872 | tf_op jit(solution)/shard_map/ijsp,djp->ijsd/dot_general | solution.py:40
  264.2 0.5 copy.62
  264.7 0.9 copy.63
  265.6 6.5 %all-to-all-start.3 = ((bf16[16,8,384]{2,1,0:T(8,128)(2,1)}), bf16[16,8,384]{2,1,0:T(8,128)(2,1)S(1)}, u32[]{:S(2)}, u32[]{:S(2)}) async-start(bf16[16,8,384]{2,1,0:T(8,128)(2,1)} %copy.63), calls=%async_computation.3 | async-start | bytes 196608 | tf_op jit(solution)/shard_map/all_to_all | solution.py:46
  272.2 0.0 all-reduce.11.cloned.1.call-start
  272.2 0.0 copy-done
  272.2 0.2 dynamic-slice_reduce_fusion
  272.4 6.4 %all-to-all-done.3 = bf16[16,8,384]{2,1,0:T(8,128)(2,1)S(1)} async-done(((bf16[16,8,384]{2,1,0:T(8,128)(2,1)}), bf16[16,8,384]{2,1,0:T(8,128)(2,1)S(1)}, u32[]{:S(2)}, u32[]{:S(2)}) %all-to-all-start.3) | async-done | bytes 98336 | tf_op jit(solution)/shard_map/all_to_all | solution.py:46
  278.8 1.8 reshape.115
  280.6 3.8 multiply_reduce_fusion.2
  284.5 0.0 copy-start.6
  284.5 16.1 %psum.62 = f32[8]{0:T(128)S(1)} all-reduce(f32[8]{0:T(128)S(1)} %get-tuple-element.15), channel_id=1, replica_groups=mesh['row'=8,'col'=16] {'row'}, use_global_device_ids=true, to_apply=%region_10.0 | all-reduce | flops 8 | bytes 64 | tf_op jit(solution)/shard_map/psum | solution.py:51
  300.6 29.9 %all-reduce.1 = (f32[8]{0:T(128)S(1)}, f32[8]{0:T(128)S(1)}) all-reduce(f32[8]{0:T(128)S(1)} %get-tuple-element.8, f32[8]{0:T(128)S(1)} %psum.62), channel_id=1, replica_groups=mesh['row'=8,'col'=16] {'col'}, use_global_device_ids=true, to_apply=%region_8.0 | all-reduce | flops 16 | bytes 128 | tf_op jit(solution)/shard_map/psum | solution.py:37
  330.5 0.0 copy-done.2
  330.5 0.0 copy-done.3
  330.5 0.1 multiply_add_fusion
  330.6 0.0 copy-start.1
  330.6 5.7 %convolution_bitcast_fusion = f32[1,2,8,512]{3,2,1,0:T(8,128)S(1)} fusion(bf16[2,512,4096]{2,1,0:T(8,128)(2,1)} %param.11, f32[8,4096]{1,0:T(8,128)S(1)} %multiply_add_fusion), kind=kOutput, calls=%fused_computation.19 | convolution fusion | flops 67141632 | bytes 8552448 | tf_op jit(solution)/shard_map/bpn,dn->bdp/dot_general | solution.py:57
  336.3 2.4 fusion.44
  338.7 0.0 all-reduce.11.cloned.1.call-update
  338.8 0.7 multiply_subtract_fusion
  339.4 151.3 %all-reduce.11.cloned.1.call-done = f32[128,4096]{1,0:T(8,128)} async-done(((f32[128,4096]{1,0:T(8,128)}), f32[128,4096]{1,0:T(8,128)}) %all-reduce.11.cloned.1.call-update) | async-done | bytes 2097168
  490.7 1.5 constant_dynamic-slice_fusion
  (10 shorter events, 0.1 us)
Async XLA Ops:
  7.2 265.1 %copy-start = (s32[16,16]{1,0:T(8,128)S(1)}, s32[16,16]{1,0:T(8,128)}, u32[]{:S(2)}) copy-start(s32[16,16]{1,0:T(8,128)} %param.12) | copy-start | bytes 3076
  7.2 16.4 %copy-start.5 = (s32[16,8]{0,1:T(8,128)S(1)}, s32[16,8]{0,1:T(8,128)}, u32[]{:S(2)}) copy-start(s32[16,8]{0,1:T(8,128)} %param.10) | copy-start | bytes 1540
  15.9 14.3 %all-to-all-start = ((bf16[16,2,1536]{2,1,0:T(2,128)(2,1)}), bf16[16,2,1536]{2,1,0:T(2,128)(2,1)S(1)}, u32[]{:S(2)}, u32[]{:S(2)}) async-start(bf16[16,2,1536]{2,1,0:T(2,128)(2,1)} %reshape.129), calls=%async_computation | async-start | bytes 196608 | tf_op jit(solution)/shard_map/all_to_all | solution.py:30
  23.5 72.1 %all-reduce.7.cloned.1.call-start = ((), (), s32[]{:S(2)}) async-start(), calls=%async_computation.4 | async-start | bytes 262144 | tf_op jit(solution)/shard_map/psum | solution.py:35
  37.4 219.7 %all-reduce.9.cloned.1.call-start = ((), (), s32[]{:S(2)}) async-start(), calls=%async_computation.5 | async-start | bytes 262144 | tf_op jit(solution)/shard_map/psum | solution.py:35
  102.6 65.6 %copy-start.4 = (f32[8,512]{1,0:T(8,128)S(1)}, f32[8,512]{1,0:T(8,128)}, u32[]{:S(2)}) copy-start(f32[8,512]{1,0:T(8,128)} %param.7) | copy-start | bytes 49156
  264.2 66.3 %copy-start.2 = (f32[8,4096]{1,0:T(8,128)S(1)}, f32[8,4096]{1,0:T(8,128)}, u32[]{:S(2)}) copy-start(f32[8,4096]{1,0:T(8,128)} %all-reduce.7.cloned.1.call-done) | copy-start | bytes 393220
  264.2 66.3 %copy-start.3 = (f32[8,4096]{1,0:T(8,128)S(1)}, f32[8,4096]{1,0:T(8,128)}, u32[]{:S(2)}) copy-start(f32[8,4096]{1,0:T(8,128)} %all-reduce.9.cloned.1.call-done) | copy-start | bytes 393220
  265.6 13.2 %all-to-all-start.3 = ((bf16[16,8,384]{2,1,0:T(8,128)(2,1)}), bf16[16,8,384]{2,1,0:T(8,128)(2,1)S(1)}, u32[]{:S(2)}, u32[]{:S(2)}) async-start(bf16[16,8,384]{2,1,0:T(8,128)(2,1)} %copy.63), calls=%async_computation.3 | async-start | bytes 196608 | tf_op jit(solution)/shard_map/all_to_all | solution.py:46
  272.2 218.5 %all-reduce.11.cloned.1.call-start = ((), (), s32[]{:S(2)}) async-start(), calls=%async_computation.6 | async-start | bytes 4194304
  284.5 51.8 %copy-start.6 = (s32[128]{0:T(128)S(1)}, s32[128]{0:T(128)}, u32[]{:S(2)}) copy-start(s32[128]{0:T(128)} %param.13) | copy-start | bytes 1540
  330.6 8.2 %copy-start.1 = (f32[8,4096]{1,0:T(8,128)}, f32[8,4096]{1,0:T(8,128)S(1)}, u32[]{:S(2)}) copy-start(f32[8,4096]{1,0:T(8,128)S(1)} %multiply_add_fusion) | copy-start | bytes 393220
Sparse Core Ops, SparseCore 0:
  37.6 58.0 all-reduce.6
  195.7 61.4 all-reduce.8
  338.9 151.7 all-reduce.10
